TPU v7x, 32 devices: a whole 2x2x4 slice. The times are simulated.
32 devices in a mesh: shard: 4 (over x, core), rep: 8 (over z, y).
Axes of the slice: x: 2, y: 2, z: 4, core: 2. Of those that a mesh axis runs over, the one named last changes fastest.
Arguments:
- tokens: bfloat16 [32, 1024, 1536], P(('shard', 'rep')), may hold values from -6 to 6
- norm_gain: bfloat16 [1536], P('shard'), may hold values from 0.5 to 1.5
- in_weight: bfloat16 [1536, 6448], P('shard'), may hold values from -0.15625 to 0.15625
- conv_weight: bfloat16 [4, 3328], P(None, 'shard'), may hold values from -0.5 to 0.5
- conv_bias: bfloat16 [3328], P('shard'), may hold values from -0.5 to 0.5
- dt_bias: bfloat16 [48], P('shard'), may hold values from -4 to -1
- a_log: bfloat16 [48], P('shard'), may hold values from -4 to 1.5
- skip: bfloat16 [48], P('shard'), may hold values from 0.5 to 1.5
- gate_gain: bfloat16 [3072], P('shard'), may hold values from 0.5 to 1.5
- out_weight: bfloat16 [3072, 1536], P('shard'), may hold values from -0.109375 to 0.109375
- cotangent: bfloat16 [32, 1024, 1536], P(('shard', 'rep')), may hold values from -6 to 6
Outputs:
- output: bfloat16 [32, 1024, 1536], P(('shard', 'rep'))
- input_grad: float32 [32, 1024, 1536], P(('shard', 'rep'))
- norm_gain_grad: float32 [1536], P('shard')
- in_weight_grad: float32 [1536, 6448], P('shard')
- conv_weight_grad: float32 [4, 3328], P(None, 'shard')
- conv_bias_grad: float32 [3328], P('shard')
- dt_bias_grad: float32 [48], P('shard')
- a_log_grad: float32 [48], P('shard')
- skip_grad: float32 [48], P('shard')
- gate_gain_grad: float32 [3072], P('shard')
- out_weight_grad: float32 [3072, 1536], P('shard')
All inputs are finite; a program needn't handle non-finite values.
Results may differ from a plain program's by a relative error of at most 0.0077.
Values may be sent and summed in bfloat16 or wider, within the bound.
No kernel may reach another device: no remote copies, remote signals or barrier semaphores. Data moves between devices by JAX's collectives and lax.ppermute only.
A program may use at most 448 MiB of HBM per device.

v0:
```python
import jax
import jax.numpy as jnp
from jax import lax
from jax.sharding import PartitionSpec as P

STRETCH = 256
epsilon = 1e-05


def rms_scale(values, gain):
    return values * lax.rsqrt(jnp.mean(values * values, axis=-1, keepdims=True) + epsilon) * gain


def stretch_step(state, values, keys_b, keys_c, steps, decay_rate):
    logs = jnp.cumsum(steps * decay_rate, axis=0)
    span = logs.shape[0]
    rows = lax.broadcasted_iota(jnp.int32, (span, span), 0)
    cols = lax.broadcasted_iota(jnp.int32, (span, span), 1)
    causal = (rows >= cols)[None, :, :]
    logs_heads = logs.T
    gaps = logs_heads[:, :, None] - logs_heads[:, None, :]
    weights = jnp.where(causal, jnp.exp(jnp.where(causal, gaps, 0.0)), 0.0)
    inner = jnp.dot(keys_c, keys_b.T, precision=lax.Precision.HIGHEST)
    mixing = inner[None, :, :] * weights * steps.T[:, None, :]
    local = jnp.einsum("hts,shp->thp", mixing, values, precision=lax.Precision.HIGHEST)
    carried = (
        jnp.einsum("hpn,tn->thp", state, keys_c, precision=lax.Precision.HIGHEST)
        * jnp.exp(logs)[:, :, None]
    )
    last = logs[-1]
    tails = jnp.exp(last[None, :] - logs) * steps
    scaled = values * tails[:, :, None]
    fresh = jnp.einsum("shp,sn->hpn", scaled, keys_b, precision=lax.Precision.HIGHEST)
    new_state = jnp.exp(last)[:, None, None] * state + fresh
    return (new_state, (local + carried).reshape(span, -1))


def mixer(proj, conv_weight, conv_bias, dt_bias, a_log, skip, gate_gain):
    length = proj.shape[0]
    inner_width = gate_gain.shape[0]
    state_size = (conv_bias.shape[0] - inner_width) // 2
    heads = dt_bias.shape[0]
    head_width = inner_width // heads
    taps = conv_weight.shape[0]
    gate = proj[:, :inner_width]
    conv_in = proj[:, inner_width : 2 * inner_width + 2 * state_size]
    raw_steps = proj[:, 2 * inner_width + 2 * state_size :]
    padded = jnp.pad(conv_in, ((taps - 1, 0), (0, 0)))
    conv_sum = jnp.zeros_like(conv_in) + conv_bias
    for offset in range(taps):
        conv_sum = conv_sum + conv_weight[offset] * padded[offset : offset + length]
    act = jax.nn.silu(conv_sum)
    values = act[:, :inner_width]
    keys_b = act[:, inner_width : inner_width + state_size]
    keys_c = act[:, inner_width + state_size :]
    steps = jax.nn.softplus(raw_steps + dt_bias)
    decay_rate = -jnp.exp(a_log)
    blocks = length // STRETCH

    def advance(state, block_values, block_b, block_c, block_steps):
        return stretch_step(
            state,
            block_values.reshape(STRETCH, heads, head_width),
            block_b,
            block_c,
            block_steps,
            decay_rate,
        )

    stepper = jax.checkpoint(advance)
    state = jnp.zeros((heads, head_width, state_size), jnp.float32)
    outputs = []
    for index in range(blocks):
        lower = index * STRETCH
        state, piece = stepper(
            state,
            values[lower : lower + STRETCH],
            keys_b[lower : lower + STRETCH],
            keys_c[lower : lower + STRETCH],
            steps[lower : lower + STRETCH],
        )
        outputs.append(piece)
    scan_flat = jnp.concatenate(outputs, axis=0)
    skip_cols = jnp.repeat(skip, head_width)
    scan_out = scan_flat + skip_cols[None, :] * values
    gated = scan_out * jax.nn.silu(gate)
    return rms_scale(gated, gate_gain)


def on_device(
    tokens,
    norm_gain,
    in_weight,
    conv_weight,
    conv_bias,
    dt_bias,
    a_log,
    skip,
    gate_gain,
    out_weight,
    cotangent,
):
    whole = (
        lax.all_gather(norm_gain, "shard", axis=0, tiled=True),
        lax.all_gather(in_weight, "shard", axis=0, tiled=True),
        lax.all_gather(conv_weight, "shard", axis=1, tiled=True),
        lax.all_gather(conv_bias, "shard", axis=0, tiled=True),
        lax.all_gather(dt_bias, "shard", axis=0, tiled=True),
        lax.all_gather(a_log, "shard", axis=0, tiled=True),
        lax.all_gather(skip, "shard", axis=0, tiled=True),
        lax.all_gather(gate_gain, "shard", axis=0, tiled=True),
        lax.all_gather(out_weight, "shard", axis=0, tiled=True),
    )
    (
        gain_full,
        in_full,
        conv_w_full,
        conv_b_full,
        dt_full,
        alog_full,
        skip_full,
        gate_full,
        out_full,
    ) = whole
    small = tuple(
        (
            item.astype(jnp.float32)
            for item in (conv_w_full, conv_b_full, dt_full, alog_full, skip_full, gate_full)
        )
    )
    seqs, length, width = tokens.shape
    total_rows = seqs * length
    flat = tokens.reshape(total_rows, width).astype(jnp.float32)
    normed_f, norm_pull = jax.vjp(rms_scale, flat, gain_full.astype(jnp.float32))
    normed = normed_f.astype(jnp.bfloat16)
    proj = jnp.dot(normed, in_full, preferred_element_type=jnp.float32)

    def mix_all(proj_rows, conv_w, conv_b, dt_b, alog_v, skip_v, gate_g):
        shaped = proj_rows.reshape(seqs, length, proj_rows.shape[1])
        mixed_rows = jax.vmap(mixer, in_axes=(0, None, None, None, None, None, None))(
            shaped, conv_w, conv_b, dt_b, alog_v, skip_v, gate_g
        )
        return mixed_rows.reshape(total_rows, mixed_rows.shape[2])

    mixed_f, mix_pull = jax.vjp(mix_all, proj, *small)
    mixed = mixed_f.astype(jnp.bfloat16)
    branch_out = jnp.dot(mixed, out_full, preferred_element_type=jnp.float32)
    output = (flat + branch_out).astype(jnp.bfloat16).reshape(seqs, length, width)
    in_back, out_back = (
        lax.all_gather(in_weight, "shard", axis=0, tiled=True),
        lax.all_gather(out_weight, "shard", axis=0, tiled=True),
    )
    cot_rows = cotangent.reshape(total_rows, width)
    mixed_grad = lax.dot_general(
        cot_rows, out_back, (((1,), (1,)), ((), ())), preferred_element_type=jnp.float32
    )
    mix_grads = mix_pull(mixed_grad)
    proj_grad = mix_grads[0].astype(jnp.bfloat16)
    normed_grad = lax.dot_general(
        proj_grad, in_back, (((1,), (1,)), ((), ())), preferred_element_type=jnp.float32
    )
    flat_grad, gain_grad = norm_pull(normed_grad)
    input_grad = (cot_rows.astype(jnp.float32) + flat_grad).reshape(seqs, length, width)
    out_grad = lax.dot_general(
        mixed, cot_rows, (((0,), (0,)), ((), ())), preferred_element_type=jnp.float32
    )
    in_grad = lax.dot_general(
        normed, proj_grad, (((0,), (0,)), ((), ())), preferred_element_type=jnp.float32
    )
    owned = (
        lax.psum_scatter(gain_grad, "shard", scatter_dimension=0, tiled=True),
        lax.psum_scatter(in_grad, "shard", scatter_dimension=0, tiled=True),
        lax.psum_scatter(mix_grads[1], "shard", scatter_dimension=1, tiled=True),
        lax.psum_scatter(mix_grads[2], "shard", scatter_dimension=0, tiled=True),
        lax.psum_scatter(mix_grads[3], "shard", scatter_dimension=0, tiled=True),
        lax.psum_scatter(mix_grads[4], "shard", scatter_dimension=0, tiled=True),
        lax.psum_scatter(mix_grads[5], "shard", scatter_dimension=0, tiled=True),
        lax.psum_scatter(mix_grads[6], "shard", scatter_dimension=0, tiled=True),
        lax.psum_scatter(out_grad, "shard", scatter_dimension=0, tiled=True),
    )
    summed = lax.psum(
        (owned[0], owned[1], owned[2], owned[3], owned[4], owned[5], owned[6], owned[7], owned[8]),
        "rep",
    )
    return (
        output,
        input_grad,
        summed[0],
        summed[1],
        summed[2],
        summed[3],
        summed[4],
        summed[5],
        summed[6],
        summed[7],
        summed[8],
    )


def solution(mesh):
    placed = (
        P(("shard", "rep"), None, None),
        P("shard"),
        P("shard", None),
        P(None, "shard"),
        P("shard"),
        P("shard"),
        P("shard"),
        P("shard"),
        P("shard"),
        P("shard", None),
        P(("shard", "rep"), None, None),
    )
    return jax.shard_map(
        on_device,
        mesh=mesh,
        in_specs=placed,
        out_specs=(
            P(("shard", "rep"), None, None),
            P(("shard", "rep"), None, None),
            P("shard"),
            P("shard", None),
            P(None, "shard"),
            P("shard"),
            P("shard"),
            P("shard"),
            P("shard"),
            P("shard"),
            P("shard", None),
        ),
        check_vma=False,
    )
```

profile of v0, /device:TPU:0, one launch (start us, length us, event | category | flops | bytes accessed | tf_op | source)
XLA Modules:
  0.0 1886.3 jit_solution(5279300305673587679)
XLA Ops:
  14.7 6.1 all-gather.1
  21.9 8.0 all-reduce.47
  30.6 5.4 all-gather.2
  37.3 5.5 all-gather
  43.6 94.0 %all-gather.6.cloned.1.call-done = bf16[1536,6448]{0,1:T(8,128)(2,1)} async-done(((bf16[384,6448]{0,1:T(8,128)(2,1)}), bf16[1536,6448]{0,1:T(8,128)(2,1)}) %all-gather.6.cloned.1.call-update) | async-done | bytes 19808272 | tf_op jit(solution)/shard_map/all_gather | solution.py:105
  137.6 29.2 %convolution_bitcast_fusion = f32[1,1024,6448]{2,1,0:T(8,128)} fusion(bf16[1536,6448]{0,1:T(8,128)(2,1)} %all-gather.6.cloned.1.call-done, bf16[1,1024,1536]{2,1,0:T(8,128)(2,1)S(1)} %copy-done.29, f32[1536]{0:T(1024)S(1)} %reshape.1986, f32[1024]{0:T(1024)S(1)} %fusion.294), kind=kOutput, calls=%fused_computation.4 | convolution fusion | flops 20289945600 | bytes 49375232 | tf_op jit(solution)/shard_map/dot_general | solution.py:136
  173.2 10.6 slice.245
  200.2 24.7 %fusion.2 = (f32[1,1024,3328]{2,1,0:T(8,128)S(1)}, f32[1,1024,3328]{2,1,0:T(8,128)}) fusion(f32[1,1024,3328]{2,1,0:T(8,128)} %slice.245, f32[3328]{0:T(1024)} %get-tuple-element.111, f32[3328]{0:T(1024)} %get-tuple-element.112, f32[3328]{0:T(1024)} %get-tuple-element.113, f32[3328]{0:T(1024)} %get-tuple-element.110, f32[3328]{0:T(1024)} %convert_element_type.62), kind=kLoop, calls=%fused_computation.15 | loop fusion | flops 40894464 | bytes 40961024 | tf_op jit(solution)/shard_map/jvp(vmap(jit(silu)))/mul | solution.py:52
  231.6 15.2 fusion.336
  279.6 17.2 bitcast_add_fusion.6
  324.3 16.2 bitcast_add_fusion.3
  352.6 17.0 bitcast_add_fusion.4
  381.9 17.1 bitcast_add_fusion.5
  402.5 18.6 multiply_reduce_fusion.13
  423.4 17.6 fusion.139
  441.0 19.8 %fusion.6 = (f32[3072]{0:T(1024)}, f32[1024]{0:T(1024)S(1)}, f32[1024,3072]{1,0:T(8,128)}) fusion(f32[1,1024,3072]{2,1,0:T(8,128)} %get-tuple-element.145, f32[1024]{0:T(1024)S(1)} %fusion.295, f32[3072]{0:T(1024)S(1)} %bitcast.1060, bf16[3072,1536]{1,0:T(8,128)(2,1)} %all-gather.8.cloned.1.call-done, bf16[1,1024,1536]{2,1,0:T(8,128)(2,1)} %param.21), kind=kOutput, calls=%fused_computation.24 | convolution fusion | flops 9682546688 | bytes 37781504 | tf_op jit(solution)/shard_map/dot_general | solution.py:154
  460.8 32.0 %multiply_reduce_fusion.4 = (f32[3072]{0:T(1024)}, f32[1,1024,3072]{2,1,0:T(8,128)}, f32[1,1024,3072]{2,1,0:T(8,128)}) fusion(f32[1,1024,3328]{2,1,0:T(8,128)} %copy-done, f32[1,1024,6448]{2,1,0:T(8,128)} %convolution_bitcast_fusion, f32[1,1024,3072]{2,1,0:T(8,128)} %get-tuple-element.145, f32[1024]{0:T(1024)S(1)} %multiply_multiply_fusion.1, ...), kind=kLoop, calls=%fused_computation.27 | loop fusion | flops 75494400 | bytes 88125440 | tf_op jit(solution)/shard_map/transpose(jvp(vmap()))/reduce_sum | solution.py:85
  492.8 9.8 fusion.337
  524.2 5.6 convolution_bitcast_fusion.1
  555.0 6.1 bitcast_add_fusion.8
  586.6 6.3 bitcast_add_fusion.7
  649.6 13.8 fusion.14
  667.1 6.4 fusion.138
  675.1 6.1 fusion.137
  682.8 6.8 fusion.136
  694.1 13.6 fusion.340
  707.8 13.1 fusion.341
  721.0 13.3 fusion.342
  734.4 46.2 %fusion.65 = (f32[48,256]{1,0:T(8,128)S(1)}, f32[48,256]{1,0:T(8,128)S(1)}, f32[48,256]{1,0:T(8,128)}, f32[256,256]{1,0:T(8,128)}, f32[256,256]{1,0:T(8,128)}, /...) fusion(f32[48,256]{1,0:T(8,128)S(1)} %copy-done.105, ...), kind=kOutput, calls=%fused_computation.108 | convolution fusion | flops 2604253184 | bytes 47185920 | tf_op jit(solution)/shard_map/transpose(jvp(vmap(jvp(vmap()))))/checkpoint/hts,shp->thp/dot_general | solution.py:25
  801.5 14.1 bitcast_add_fusion.2
  835.1 14.0 bitcast_add_fusion.1
  874.2 14.0 bitcast_add_fusion
  945.4 7.4 fusion.214
  959.9 5.5 fusion.196
  984.5 5.4 fusion.193
  992.8 10.0 pad_add_fusion.3
  1002.8 36.0 %multiply_reduce_fusion.2 = (f32[3328]{0:T(1024)S(1)}, f32[3328]{0:T(1024)S(1)}, f32[3328]{0:T(1024)S(1)}, f32[3328]{0:T(1024)}, f32[3328]{0:T(1024)S(1)}, /*index=5*/f32[1,1024,3328]{2,1,0:T(8,128)}) fusion(f32[1,1024,3328]{2,1,0:T(8,128)} %slice.245, f32[1,1024,6448]{2,1,0:T(8,128)} %convolution_bitcast_fusion, f32[1,1024,3328]{2,1,0:T(8,128)} %get-tuple-element.153, ...), kind=kLoop, calls=%fused_computation.12 | loop fusion | flops 68140800 | bytes 68224000 | tf_op jit(solution)/shard_map/transpose(jvp(vmap()))/reduce_sum | solution.py:51
  1038.8 17.1 broadcast_multiply_fusion
  1055.9 19.7 %pad_add_fusion = f32[1,1024,3328]{2,1,0:T(8,128)} fusion(f32[1,1024,3328]{2,1,0:T(8,128)} %get-tuple-element.156, f32[1,1024,3328]{2,1,0:T(8,128)} %get-tuple-element.157, f32[1,1024,3328]{2,1,0:T(8,128)} %get-tuple-element.158, f32[1,1024,3328]{2,1,0:T(8,128)S(1)} %get-tuple-element.155), kind=kLoop, calls=%fused_computation.7 | loop fusion | flops 10223616 | bytes 68157440 | tf_op jit(solution)/shard_map/transpose(jvp(vmap()))/add_any | solution.py:51
  1075.6 33.5 %fusion.133 = f32[1536,6448]{0,1:T(8,128)} fusion(bf16[1,1024,1536]{2,1,0:T(8,128)(2,1)S(1)} %copy-done.30, f32[1536]{0:T(1024)S(1)} %copy-done.125, f32[1024]{0:T(1024)S(1)} %copy-done.129, f32[1,1024,3072]{2,1,0:T(8,128)} %get-tuple-element.154, f32[1,1024,3328]{2,1,0:T(8,128)} %pad_add_fusion, f32[1,1024,48]{2,1,0:T(8,128)} %get-tuple-element.136), kind=kOutput, calls=%fused_computation.176 | convolution fusion | flops 20309753856 | bytes 69183488 | tf_op jit(solution)/shard_map/dot_general | solution.py:167
  1111.1 267.0 %reduce-scatter.6.cloned.1.call-done = f32[384,6448]{0,1:T(8,128)} async-done(((f32[1536,6448]{0,1:T(8,128)}), f32[384,6448]{0,1:T(8,128)}) %reduce-scatter.6.cloned.1.call-update) | async-done | bytes 9904144 | tf_op jit(solution)/shard_map/reduce_scatter | solution.py:172
  1381.0 33.0 %fusion.73 = (f32[1536]{0:T(1024)S(1)}, f32[1024]{0:T(1024)S(1)}, f32[1024,1536]{1,0:T(8,128)}) fusion(bf16[1,1024,1536]{2,1,0:T(8,128)(2,1)S(1)} %copy-done.30, f32[1024]{0:T(1024)S(1)} %copy-done.129, f32[1536]{0:T(1024)S(1)} %copy-done.125, bf16[1536,6448]{0,1:T(8,128)(2,1)} %all-gather.6.cloned.1.call-done, f32[1,1024,3072]{2,1,0:T(8,128)} %get-tuple-element.154, ...), kind=kOutput, calls=%fused_computation.116 | convolution fusion | flops 20314468352 | bytes 55676928 | tf_op jit(solution)/shard_map/dot_general | solution.py:159
  1414.0 11.1 all-reduce.46
  1425.7 6.4 fusion.80
  1432.0 17.0 fusion.131
  1450.2 40.2 %all-reduce.44 = (f32[384]{0:T(512)}, f32[4,832]{1,0:T(4,128)}, f32[832]{0:T(1024)}, f32[12]{0:T(128)}, f32[12]{0:T(128)}, /*index=5*/f32[12]{0:T(128)}, f32[768]{0:T(1024)}) all-reduce(f32[384]{0:T(512)S(1)} %dynamic-slice.5, f32[4,832]{1,0:T(4,128)S(1)} %copy.695, ...), channel_id=1, replica_groups=mesh['shard'=4,'rep'=8] {'rep'}, use_global_device_ids=true, to_apply=%region_59.60 | all-reduce | flops 5348 | bytes 42784 | tf_op jit(solution)/shard_map/psum | solution.py:181
  1490.4 378.2 %all-reduce.50.cloned.1.call-done = (f32[384,6448]{0,1:T(8,128)}, f32[768,1536]{1,0:T(8,128)}) async-done(((f32[384,6448]{0,1:T(8,128)}, f32[768,1536]{1,0:T(8,128)}), (f32[384,6448]{0,1:T(8,128)}, f32[768,1536]{1,0:T(8,128)})) %all-reduce.50.cloned.1.call-update) | async-done | bytes 14622736 | tf_op jit(solution)/shard_map/psum | solution.py:181
  1868.6 8.5 copy.728
  (631 shorter events, 426.6 us)
Async XLA Ops:
  7.2 30.1 %copy-start.133 = (bf16[4,832]{1,0:T(4,128)(2,1)S(1)}, bf16[4,832]{1,0:T(4,128)(2,1)}, u32[]{:S(2)}) copy-start(bf16[4,832]{1,0:T(4,128)(2,1)} %param.14) | copy-start | bytes 19972
  7.2 130.3 %all-gather.6.cloned.1.call-start = ((), (), s32[]{:S(2)}) async-start(), calls=%async_computation.3 | async-start | bytes 24760320 | tf_op jit(solution)/shard_map/all_gather | solution.py:105
  8.0 433.0 %all-gather.8.cloned.1.call-start = ((), (), s32[]{:S(2)}) async-start(), calls=%async_computation.4 | async-start | bytes 11796480 | tf_op jit(solution)/shard_map/all_gather | solution.py:112
  8.7 1102.4 %reduce-scatter.8.cloned.1.call-start = ((), (), s32[]{:S(2)}) async-start(), calls=%async_computation.6 | async-start | bytes 23592960 | tf_op jit(solution)/shard_map/reduce_scatter | solution.py:179
  14.7 152.1 %copy-start.128 = (f32[1024]{0:T(1024)}, f32[1024]{0:T(1024)S(1)}, u32[]{:S(2)}) copy-start(f32[1024]{0:T(1024)S(1)} %fusion.294) | copy-start | bytes 12292
  20.9 145.9 %copy-start.124 = (f32[1536]{0:T(1024)}, f32[1536]{0:T(1024)S(1)}, u32[]{:S(2)}) copy-start(f32[1536]{0:T(1024)S(1)} %reshape.1986) | copy-start | bytes 18436
  29.9 138.2 %copy-start.119 = (f32[48]{0:T(128)}, f32[48]{0:T(128)S(1)}, u32[]{:S(2)}) copy-start(f32[48]{0:T(128)S(1)} %fusion.296) | copy-start | bytes 580
  29.9 136.9 %copy-start.134 = (f32[48]{0:T(128)}, f32[48]{0:T(128)S(1)}, u32[]{:S(2)}) copy-start(f32[48]{0:T(128)S(1)} %convert_element_type.66) | copy-start | bytes 580
  200.2 30.6 %copy-start.95 = (f32[48,2]{1,0:T(8,128)S(1)}, f32[48,2]{1,0:T(8,128)}, u32[]{:S(2)}) copy-start(f32[48,2]{1,0:T(8,128)} %copy.584) | copy-start | bytes 1156
  200.2 31.4 %copy-start.82 = (f32[1,48,2,128]{3,2,0,1:T(2,128)S(1)}, f32[1,48,2,128]{3,2,0,1:T(2,128)}, u32[]{:S(2)}) copy-start(f32[1,48,2,128]{3,2,0,1:T(2,128)} %copy.589) | copy-start | bytes 147460
  246.8 26.7 %copy-start.7 = (f32[1,256,3072]{2,1,0:T(8,128)}, f32[1,256,3072]{2,1,0:T(8,128)S(1)}, u32[]{:S(2)}) copy-start(f32[1,256,3072]{2,1,0:T(8,128)S(1)} %get-tuple-element.67) | copy-start | bytes 9437188
  310.6 320.8 %copy-start.1 = (f32[48,64,128]{2,1,0:T(8,128)}, f32[48,64,128]{2,1,0:T(8,128)S(1)}, u32[]{:S(2)}) copy-start(f32[48,64,128]{2,1,0:T(8,128)S(1)} %convolution_add_fusion) | copy-start | bytes 4718596
  315.7 296.4 %copy-start.3 = (f32[48,64,128]{2,1,0:T(8,128)}, f32[48,64,128]{2,1,0:T(8,128)S(1)}, u32[]{:S(2)}) copy-start(f32[48,64,128]{2,1,0:T(8,128)S(1)} %multiply_add_fusion.2) | copy-start | bytes 4718596
  421.2 39.7 %copy-start.126 = (f32[1024]{0:T(1024)}, f32[1024]{0:T(1024)S(1)}, u32[]{:S(2)}) copy-start(f32[1024]{0:T(1024)S(1)} %fusion.295) | copy-start | bytes 12292
  423.4 100.8 %copy-start.44 = (f32[1,256,128]{2,1,0:T(8,128)}, f32[1,256,128]{2,1,0:T(8,128)S(1)}, u32[]{:S(2)}) copy-start(f32[1,256,128]{2,1,0:T(8,128)S(1)} %get-tuple-element.42) | copy-start | bytes 393220
  423.4 131.6 %copy-start.41 = (f32[1,256,128]{2,1,0:T(8,128)}, f32[1,256,128]{2,1,0:T(8,128)S(1)}, u32[]{:S(2)}) copy-start(f32[1,256,128]{2,1,0:T(8,128)S(1)} %get-tuple-element.54) | copy-start | bytes 393220
  601.1 777.1 %reduce-scatter.6.cloned.1.call-start = ((), (), s32[]{:S(2)}) async-start(), calls=%async_computation.5 | async-start | bytes 49520640 | tf_op jit(solution)/shard_map/reduce_scatter | solution.py:172
  691.1 43.1 %copy-start.106 = (f32[48,256]{1,0:T(8,128)}, f32[48,256]{1,0:T(8,128)S(1)}, u32[]{:S(2)}) copy-start(f32[48,256]{1,0:T(8,128)S(1)} %bitcast_add_fusion.28) | copy-start | bytes 147460
  692.0 42.3 %copy-start.104 = (f32[48,256]{1,0:T(8,128)}, f32[48,256]{1,0:T(8,128)S(1)}, u32[]{:S(2)}) copy-start(f32[48,256]{1,0:T(8,128)S(1)} %bitcast_add_fusion.27) | copy-start | bytes 147460
  692.9 41.4 %copy-start.102 = (f32[48,256]{1,0:T(8,128)}, f32[48,256]{1,0:T(8,128)S(1)}, u32[]{:S(2)}) copy-start(f32[48,256]{1,0:T(8,128)S(1)} %bitcast_add_fusion.26) | copy-start | bytes 147460
  693.3 41.0 %copy-start.79 = (f32[256,256]{1,0:T(8,128)}, f32[256,256]{1,0:T(8,128)S(1)}, u32[]{:S(2)}) copy-start(f32[256,256]{1,0:T(8,128)S(1)} %fusion.255) | copy-start | bytes 786436
  693.7 40.6 %copy-start.77 = (f32[256,256]{1,0:T(8,128)}, f32[256,256]{1,0:T(8,128)S(1)}, u32[]{:S(2)}) copy-start(f32[256,256]{1,0:T(8,128)S(1)} %fusion.244) | copy-start | bytes 786436
  694.1 40.2 %copy-start.76 = (f32[256,256]{1,0:T(8,128)}, f32[256,256]{1,0:T(8,128)S(1)}, u32[]{:S(2)}) copy-start(f32[256,256]{1,0:T(8,128)S(1)} %fusion.233) | copy-start | bytes 786436
  734.4 46.3 %copy-start.20 = (f32[48,64,128]{2,1,0:T(8,128)S(1)}, f32[48,64,128]{2,1,0:T(8,128)}, u32[]{:S(2)}) copy-start(f32[48,64,128]{2,1,0:T(8,128)} %copy-done.19) | copy-start | bytes 4718596
  734.4 46.3 %copy-start.45 = (f32[1,256,128]{2,1,0:T(8,128)S(1)}, f32[1,256,128]{2,1,0:T(8,128)}, u32[]{:S(2)}) copy-start(f32[1,256,128]{2,1,0:T(8,128)} %copy-done.44) | copy-start | bytes 393220
  734.4 49.0 %copy-start.71 = (f32[1,256,48]{1,0,2:T(1,128)S(1)}, f32[1,256,48]{1,0,2:T(1,128)}, u32[]{:S(2)}) copy-start(f32[1,256,48]{1,0,2:T(1,128)} %copy-done.70) | copy-start | bytes 147460
  734.4 59.7 %copy-start.51 = (f32[1,48,256]{1,2,0:T(8,128)S(1)}, f32[1,48,256]{1,2,0:T(8,128)}, u32[]{:S(2)}) copy-start(f32[1,48,256]{1,2,0:T(8,128)} %copy-done.50) | copy-start | bytes 147460
  734.4 59.7 %copy-start.37 = (f32[1,256,48]{2,1,0:T(8,128)S(1)}, f32[1,256,48]{2,1,0:T(8,128)}, u32[]{:S(2)}) copy-start(f32[1,256,48]{2,1,0:T(8,128)} %get-tuple-element.49) | copy-start | bytes 147460
  734.4 60.7 %copy-start.4 = (f32[48,64,128]{2,1,0:T(8,128)S(1)}, f32[48,64,128]{2,1,0:T(8,128)}, u32[]{:S(2)}) copy-start(f32[48,64,128]{2,1,0:T(8,128)} %copy-done.3) | copy-start | bytes 4718596
  936.4 29.0 %copy-start.55 = (f32[1,256,128]{2,1,0:T(8,128)S(1)}, f32[1,256,128]{2,1,0:T(8,128)}, u32[]{:S(2)}) copy-start(f32[1,256,128]{2,1,0:T(8,128)} %get-tuple-element.53) | copy-start | bytes 393220
  936.4 29.0 %copy-start.66 = (f32[256,256]{1,0:T(8,128)S(1)}, f32[256,256]{1,0:T(8,128)}, u32[]{:S(2)}) copy-start(f32[256,256]{1,0:T(8,128)} %get-tuple-element.98) | copy-start | bytes 786436
  939.9 25.9 %copy-start.12 = (f32[1,256,3072]{1,2,0:T(8,128)S(1)}, f32[1,256,3072]{1,2,0:T(8,128)}, u32[]{:S(2)}) copy-start(f32[1,256,3072]{1,2,0:T(8,128)} %copy.606) | copy-start | bytes 9437188
  939.9 25.9 %copy-start.21 = (f32[48,64,128]{2,1,0:T(8,128)S(1)}, f32[48,64,128]{2,1,0:T(8,128)}, u32[]{:S(2)}) copy-start(f32[48,64,128]{2,1,0:T(8,128)} %copy-done.19) | copy-start | bytes 4718596
  965.9 26.9 %slice-start = ((s8[12582912]{0:T(1024)(128)(4,1)}), s8[4194304]{0:T(1024)(128)(4,1)S(1)}, s32[]{:S(2)}) async-start(s8[12582912]{0:T(1024)(128)(4,1)} %bitcast.941), calls=%async_computation.9 | async-start | bytes 8388608
  1002.8 36.0 %copy-start.91 = (f32[3328]{0:T(1024)S(1)}, f32[3328]{0:T(1024)}, u32[]{:S(2)}) copy-start(f32[3328]{0:T(1024)} %get-tuple-element.110) | copy-start | bytes 39940
  1002.8 36.0 %copy-start.92 = (f32[3328]{0:T(1024)S(1)}, f32[3328]{0:T(1024)}, u32[]{:S(2)}) copy-start(f32[3328]{0:T(1024)} %get-tuple-element.111) | copy-start | bytes 39940
  1002.8 36.0 %copy-start.93 = (f32[3328]{0:T(1024)S(1)}, f32[3328]{0:T(1024)}, u32[]{:S(2)}) copy-start(f32[3328]{0:T(1024)} %get-tuple-element.112) | copy-start | bytes 39940
  1002.8 36.0 %copy-start.94 = (f32[3328]{0:T(1024)S(1)}, f32[3328]{0:T(1024)}, u32[]{:S(2)}) copy-start(f32[3328]{0:T(1024)} %get-tuple-element.113) | copy-start | bytes 39940
  1109.1 271.7 %copy-start.118 = (f32[3072]{0:T(1024)S(1)}, f32[3072]{0:T(1024)}, u32[]{:S(2)}) copy-start(f32[3072]{0:T(1024)} %get-tuple-element.133) | copy-start | bytes 36868
  1109.1 271.9 %copy-start.138 = (f32[48]{0:T(128)S(1)}, f32[48]{0:T(128)}, u32[]{:S(2)}) copy-start(f32[48]{0:T(128)} %get-tuple-element.201) | copy-start | bytes 580
  1109.1 271.9 %copy-start.139 = (f32[48]{0:T(128)S(1)}, f32[48]{0:T(128)}, u32[]{:S(2)}) copy-start(f32[48]{0:T(128)} %get-tuple-element.199) | copy-start | bytes 580
  1109.1 271.9 %copy-start.141 = (bf16[48]{0:T(256)(128)(2,1)S(1)}, bf16[48]{0:T(256)(128)(2,1)}, u32[]{:S(2)}) copy-start(bf16[48]{0:T(256)(128)(2,1)} %copy-done.140) | copy-start | bytes 292
  1109.1 340.0 %reduce-scatter.10.cloned.1.call-start = ((), (), s32[]{:S(2)}) async-start(), calls=%async_computation.7 | async-start | bytes 2129920
  1111.0 757.6 %all-reduce.50.cloned.1.call-start = ((), (), s32[]{:S(2)}) async-start(), calls=%async_computation.8 | async-start | bytes 29245440 | tf_op jit(solution)/shard_map/psum | solution.py:181
  1381.0 33.0 %copy-start.98 = (f32[3328]{0:T(1024)S(1)}, f32[3328]{0:T(1024)}, u32[]{:S(2)}) copy-start(f32[3328]{0:T(1024)} %get-tuple-element.78) | copy-start | bytes 39940
  1381.0 33.0 %copy-start.130 = (f32[3072]{0:T(1024)S(1)}, f32[3072]{0:T(1024)}, u32[]{:S(2)}) copy-start(f32[3072]{0:T(1024)} %get-tuple-element.76) | copy-start | bytes 36868
  1381.0 33.0 %copy-start.136 = (f32[48]{0:T(128)S(1)}, f32[48]{0:T(128)}, u32[]{:S(2)}) copy-start(f32[48]{0:T(128)} %get-tuple-element.135) | copy-start | bytes 580
  1381.0 44.6 %copy-start.123 = (f32[1024]{0:T(1024)S(1)}, f32[1024]{0:T(1024)}, u32[]{:S(2)}) copy-start(f32[1024]{0:T(1024)} %copy-done.122) | copy-start | bytes 12292
  (106 other events, 1404.9 us)
Sparse Core Ops, SparseCore 0:
  9.6 127.9 all-gather.5
  139.1 64.2 all-gather.7
  601.2 137.8 reduce-scatter.7
  1109.2 268.9 reduce-scatter.5
  1381.1 28.7 reduce-scatter.9
  1414.1 454.4 all-reduce.49
where the time goes:
time: 1890 us
  waiting for transfers between devices  741 us (39%)
  matrix products  494 us (26%)
  local copies, waits for them, and re-layouts  285 us (15%)
  other arithmetic  270 us (14%)
  blocking collectives  76.3 us (4%)
  between operations  20.3 us (1%)
    psum x1, waiting for transfers between devices, on_device(): lax.psum((owned[0], owned[1], owned[2], owned[3], owned[4], owned[5], own...  378 us
    reduce_scatter x1, waiting for transfers between devices, on_device(): lax.psum_scatter(in_grad, 'shard', scatter_dimension=0, tiled=True)  267 us
    dot_general x12, matrix products, stretch_step(): jnp.einsum('hts,shp->thp', mixing, values, precision=lax.Precision.HIGHEST)  210 us
    all_gather x1, waiting for transfers between devices, on_device(): lax.all_gather(in_weight, 'shard', axis=0, tiled=True)  94 us
    dot_general x15, matrix products, stretch_step(): jnp.einsum('hpn,tn->thp', state, keys_c, precision=lax.Precision.HIGHEST)  72.1 us
    mul x24, local copies, waits for them, and re-layouts, stretch_step(): scaled = values * tails[:, :, None]  56.4 us
    dot_general x9, matrix products, stretch_step(): jnp.einsum('shp,sn->hpn', scaled, keys_b, precision=lax.Precision.HIGHEST)  48.5 us
    psum x1, blocking collectives, on_device(): lax.psum((owned[0], owned[1], owned[2], owned[3], owned[4], owned[5], own...  40.2 us
  transfers between devices with their start and end apart: 6, of which 3 were waited for; matrix products, arithmetic and copies ran while one was open for 46% of the time, Pallas kernels for 0%

commit v1 on v0

--- a/solution.py
+++ b/solution.py
@@ -2,6 +2,7 @@
 import jax.numpy as jnp
 from jax import lax
 from jax.sharding import PartitionSpec as P
+from jax.lax import axis_index, axis_size, ppermute
 
 STRETCH = 256
 epsilon = 1e-05
@@ -100,9 +101,32 @@
     out_weight,
     cotangent,
 ):
+
+    def save_the_joints(sample, ax_name):
+        opened = axis_size(ax_name)
+        q_next, left_arr, wide_out = (opened, axis_index(ax_name), sample.shape[0])
+        leaves = tuple((at * q_next if u == 0 else at for u, at in enumerate(sample.shape)))
+        out_arr = jnp.zeros(leaves, sample.dtype)
+        near = lax.dynamic_update_slice_in_dim(out_arr, sample, left_arr * wide_out, axis=0)
+        tall = w2 = sample
+        for nth in range(1, q_next // 2 + 1):
+            state_next = tuple(((u, (u + 1) % q_next) for u in range(q_next)))
+            tall = ppermute(tall, ax_name, perm=state_next)
+            near = lax.dynamic_update_slice_in_dim(
+                near, tall, (left_arr - nth) % q_next * wide_out, axis=0
+            )
+            if 2 * nth < q_next:
+                w2 = ppermute(
+                    w2, ax_name, perm=tuple(((u, (u - 1) % q_next) for u in range(q_next)))
+                )
+                near = lax.dynamic_update_slice_in_dim(
+                    near, w2, (left_arr + nth) % q_next * wide_out, axis=0
+                )
+        return near
+
     whole = (
         lax.all_gather(norm_gain, "shard", axis=0, tiled=True),
-        lax.all_gather(in_weight, "shard", axis=0, tiled=True),
+        save_the_joints(in_weight, "shard"),
         lax.all_gather(conv_weight, "shard", axis=1, tiled=True),
         lax.all_gather(conv_bias, "shard", axis=0, tiled=True),
         lax.all_gather(dt_bias, "shard", axis=0, tiled=True),

time: 1890 us -> 2160 us (1.14)
  waiting for transfers between devices: 741 us -> 877 us
  blocking collectives: 76.3 us -> 174 us
  local copies, waits for them, and re-layouts: 285 us -> 313 us
    ppermute x0 -> x3, waiting for transfers between devices: none -> 105 us  [the longest x2 105 us: save_the_joints(): tall = ppermute(tall, ax_name, perm=state_next)]
    all_gather x1, blocking collectives: 6.14 us -> 101 us  [on_device(): lax.all_gather(norm_gain, 'shard', axis=0, tiled=True)]
    all_gather x1, waiting for transfers between devices: 94 us -> 125 us  [on_device(): lax.all_gather(in_weight, 'shard', axis=0, tiled=True)]
  transfers between devices with their start and end apart: 6 -> 9, of which waited for: 3 -> 5; matrix products, arithmetic and copies ran while one was open for 46% -> 49% of each run, Pallas kernels for 0% -> 0%
where the time goes in v1:
time: 2160 us
  waiting for transfers between devices  877 us (41%)
  matrix products  494 us (23%)
  local copies, waits for them, and re-layouts  313 us (14%)
  other arithmetic  274 us (13%)
  blocking collectives  174 us (8%)
    psum x1, waiting for transfers between devices, on_device(): lax.psum((owned[0], owned[1], owned[2], owned[3], owned[4], owned[5], own...  368 us
    reduce_scatter x1, waiting for transfers between devices, on_device(): lax.psum_scatter(in_grad, 'shard', scatter_dimension=0, tiled=True)  266 us
    dot_general x12, matrix products, stretch_step(): jnp.einsum('hts,shp->thp', mixing, values, precision=lax.Precision.HIGHEST)  210 us
    all_gather x1, waiting for transfers between devices, on_device(): lax.all_gather(in_weight, 'shard', axis=0, tiled=True)  125 us
    ppermute x2, waiting for transfers between devices, save_the_joints(): tall = ppermute(tall, ax_name, perm=state_next)  105 us
    all_gather x1, blocking collectives, on_device(): lax.all_gather(norm_gain, 'shard', axis=0, tiled=True)  101 us
    dot_general x15, matrix products, stretch_step(): jnp.einsum('hpn,tn->thp', state, keys_c, precision=lax.Precision.HIGHEST)  71.3 us
    mul x24, local copies, waits for them, and re-layouts, stretch_step(): scaled = values * tails[:, :, None]  56.3 us
  transfers between devices with their start and end apart: 9, of which 5 were waited for; matrix products, arithmetic and copies ran while one was open for 49% of the time, Pallas kernels for 0%

profile of v1, /device:TPU:0, one launch (start us, length us, event | category | flops | bytes accessed | tf_op | source)
XLA Modules:
  0.0 2157.4 jit_solution(5344817318151527429)
XLA Ops:
  9.7 105.0 %collective-permute-done = bf16[384,6448]{0,1:T(8,128)(2,1)} collective-permute-done((bf16[384,6448]{0,1:T(8,128)(2,1)}, bf16[384,6448]{0,1:T(8,128)(2,1)}, u32[]{:S(2)}, u32[]{:S(2)}) %collective-permute-start) | collective-permute-done | bytes 4952096 | tf_op jit(solution)/shard_map/ppermute | solution.py:114
  121.3 101.2 %all-gather.1 = bf16[4,1,384]{2,1,0:T(2,128)(2,1)S(1)} all-gather(bf16[1,1,384]{2,1,0:T(2,128)(2,1)S(1)} %reshape.1982), channel_id=1, replica_groups=mesh['shard'=4,'rep'=8] {'shard'}, dimensions={0}, use_global_device_ids=true | all-gather | bytes 3840 | tf_op jit(solution)/shard_map/all_gather | solution.py:128
  226.0 10.5 all-reduce.47
  253.9 7.2 broadcast_in_dim.307
  280.0 29.2 %convolution_bitcast_fusion = f32[1,1024,6448]{2,1,0:T(8,128)} fusion(bf16[1536,6448]{0,1:T(8,128)(2,1)} %constant_dynamic-update-slice_fusion, bf16[1,1024,1536]{2,1,0:T(8,128)(2,1)S(1)} %copy-done.29, f32[1536]{0:T(1024)S(1)} %reshape.1986, f32[1024]{0:T(1024)S(1)} %fusion.294), kind=kOutput, calls=%fused_computation.4 | convolution fusion | flops 20289945600 | bytes 49375232 | tf_op jit(solution)/shard_map/dot_general | solution.py:160
  315.7 10.6 slice.245
  342.5 25.1 %fusion.2 = (f32[1,1024,3328]{2,1,0:T(8,128)S(1)}, f32[1,1024,3328]{2,1,0:T(8,128)}) fusion(f32[1,1024,3328]{2,1,0:T(8,128)} %slice.245, f32[3328]{0:T(1024)} %get-tuple-element.111, f32[3328]{0:T(1024)} %get-tuple-element.112, f32[3328]{0:T(1024)} %get-tuple-element.113, f32[3328]{0:T(1024)} %get-tuple-element.110, f32[3328]{0:T(1024)} %convert_element_type.62), kind=kLoop, calls=%fused_computation.15 | loop fusion | flops 40894464 | bytes 40961024 | tf_op jit(solution)/shard_map/jvp(vmap(jit(silu)))/mul | solution.py:53
  374.3 15.0 fusion.336
  422.1 17.2 bitcast_add_fusion.6
  466.6 16.4 bitcast_add_fusion.3
  495.1 17.0 bitcast_add_fusion.4
  524.3 17.1 bitcast_add_fusion.5
  544.9 18.6 multiply_reduce_fusion.13
  565.8 17.3 fusion.139
  583.2 22.4 %fusion.6 = (f32[3072]{0:T(1024)}, f32[1024]{0:T(1024)S(1)}, f32[1024,3072]{1,0:T(8,128)}) fusion(f32[1,1024,3072]{2,1,0:T(8,128)} %get-tuple-element.145, f32[1024]{0:T(1024)S(1)} %fusion.295, f32[3072]{0:T(1024)S(1)} %bitcast.1062, bf16[3072,1536]{1,0:T(8,128)(2,1)} %all-gather.6.cloned.1.call-done, bf16[1,1024,1536]{2,1,0:T(8,128)(2,1)} %param.21), kind=kOutput, calls=%fused_computation.24 | convolution fusion | flops 9682546688 | bytes 37781504 | tf_op jit(solution)/shard_map/dot_general | solution.py:178
  605.6 33.0 %multiply_reduce_fusion.4 = (f32[3072]{0:T(1024)}, f32[1,1024,3072]{2,1,0:T(8,128)}, f32[1,1024,3072]{2,1,0:T(8,128)}) fusion(f32[1,1024,3328]{2,1,0:T(8,128)} %copy-done, f32[1,1024,6448]{2,1,0:T(8,128)} %convolution_bitcast_fusion, f32[1,1024,3072]{2,1,0:T(8,128)} %get-tuple-element.145, f32[1024]{0:T(1024)S(1)} %multiply_multiply_fusion.1, ...), kind=kLoop, calls=%fused_computation.27 | loop fusion | flops 75494400 | bytes 88125440 | tf_op jit(solution)/shard_map/transpose(jvp(vmap()))/reduce_sum | solution.py:86
  638.6 10.0 fusion.337
  670.6 5.7 convolution_bitcast_fusion.1
  701.7 6.1 bitcast_add_fusion.8
  733.3 6.2 bitcast_add_fusion.7
  794.4 13.9 fusion.14
  812.1 6.0 fusion.138
  819.7 6.0 fusion.137
  827.3 6.7 fusion.136
  838.6 13.7 fusion.340
  852.3 13.1 fusion.341
  865.6 13.2 fusion.342
  879.0 46.2 %fusion.65 = (f32[48,256]{1,0:T(8,128)S(1)}, f32[48,256]{1,0:T(8,128)S(1)}, f32[48,256]{1,0:T(8,128)}, f32[256,256]{1,0:T(8,128)}, f32[256,256]{1,0:T(8,128)}, /...) fusion(f32[48,256]{1,0:T(8,128)S(1)} %copy-done.105, ...), kind=kOutput, calls=%fused_computation.108 | convolution fusion | flops 2604253184 | bytes 47185920 | tf_op jit(solution)/shard_map/transpose(jvp(vmap(jvp(vmap()))))/checkpoint/hts,shp->thp/dot_general | solution.py:26
  945.8 14.1 bitcast_add_fusion.2
  979.4 14.0 bitcast_add_fusion.1
  1018.8 14.0 bitcast_add_fusion
  1090.0 7.4 fusion.214
  1118.3 5.6 fusion.211
  1137.4 10.1 pad_add_fusion.3
  1147.5 36.1 %multiply_reduce_fusion.2 = (f32[3328]{0:T(1024)S(1)}, f32[3328]{0:T(1024)S(1)}, f32[3328]{0:T(1024)S(1)}, f32[3328]{0:T(1024)}, f32[3328]{0:T(1024)S(1)}, /*index=5*/f32[1,1024,3328]{2,1,0:T(8,128)}) fusion(f32[1,1024,3328]{2,1,0:T(8,128)} %slice.245, f32[1,1024,6448]{2,1,0:T(8,128)} %convolution_bitcast_fusion, f32[1,1024,3328]{2,1,0:T(8,128)} %get-tuple-element.153, ...), kind=kLoop, calls=%fused_computation.12 | loop fusion | flops 68140800 | bytes 68224000 | tf_op jit(solution)/shard_map/transpose(jvp(vmap()))/reduce_sum | solution.py:52
  1183.6 17.1 broadcast_multiply_fusion
  1200.7 19.7 pad_add_fusion
  1220.4 33.2 %fusion.133 = f32[1536,6448]{0,1:T(8,128)} fusion(bf16[1,1024,1536]{2,1,0:T(8,128)(2,1)S(1)} %copy-done.30, f32[1536]{0:T(1024)S(1)} %copy-done.125, f32[1024]{0:T(1024)S(1)} %copy-done.129, f32[1,1024,3072]{2,1,0:T(8,128)} %get-tuple-element.154, f32[1,1024,3328]{2,1,0:T(8,128)} %pad_add_fusion, f32[1,1024,48]{2,1,0:T(8,128)} %get-tuple-element.136), kind=kOutput, calls=%fused_computation.176 | convolution fusion | flops 20309753856 | bytes 69183488 | tf_op jit(solution)/shard_map/dot_general | solution.py:191
  1256.3 266.5 %reduce-scatter.6.cloned.1.call-done = f32[384,6448]{0,1:T(8,128)} async-done(((f32[1536,6448]{0,1:T(8,128)}), f32[384,6448]{0,1:T(8,128)}) %reduce-scatter.6.cloned.1.call-update) | async-done | bytes 9904144 | tf_op jit(solution)/shard_map/reduce_scatter | solution.py:196
  1525.7 17.4 fusion.131
  1543.1 11.5 reduce-scatter.10.cloned.1.call-done
  1555.8 125.1 %all-gather.8.cloned.1.call-done = bf16[1536,6448]{0,1:T(8,128)(2,1)} async-done(((bf16[384,6448]{0,1:T(8,128)(2,1)}), bf16[1536,6448]{0,1:T(8,128)(2,1)}) %all-gather.8.cloned.1.call-update) | async-done | bytes 19808272 | tf_op jit(solution)/shard_map/all_gather | solution.py:174
  1680.9 32.1 %fusion.73 = (f32[1536]{0:T(1024)S(1)}, f32[1024]{0:T(1024)S(1)}, f32[1024,1536]{1,0:T(8,128)}) fusion(bf16[1,1024,1536]{2,1,0:T(8,128)(2,1)S(1)} %copy-done.30, f32[1024]{0:T(1024)S(1)} %copy-done.129, f32[1536]{0:T(1024)S(1)} %copy-done.125, bf16[1536,6448]{0,1:T(8,128)(2,1)} %all-gather.8.cloned.1.call-done, f32[1,1024,3072]{2,1,0:T(8,128)} %get-tuple-element.154, ...), kind=kOutput, calls=%fused_computation.116 | convolution fusion | flops 20314468352 | bytes 55676928 | tf_op jit(solution)/shard_map/dot_general | solution.py:183
  1713.1 11.5 all-reduce.46
  1725.1 40.2 %all-reduce.44 = (f32[384]{0:T(512)}, f32[4,832]{1,0:T(4,128)}, f32[832]{0:T(1024)}, f32[12]{0:T(128)}, f32[12]{0:T(128)}, /*index=5*/f32[12]{0:T(128)}, f32[768]{0:T(1024)}) all-reduce(f32[384]{0:T(512)S(1)} %dynamic-slice.5, f32[4,832]{1,0:T(4,128)S(1)} %copy.695, ...), channel_id=1, replica_groups=mesh['shard'=4,'rep'=8] {'rep'}, use_global_device_ids=true, to_apply=%region_59.60 | all-reduce | flops 5348 | bytes 42784 | tf_op jit(solution)/shard_map/psum | solution.py:205
  1765.3 6.4 fusion.80
  1771.7 367.8 %all-reduce.50.cloned.1.call-done = (f32[384,6448]{0,1:T(8,128)}, f32[768,1536]{1,0:T(8,128)}) async-done(((f32[384,6448]{0,1:T(8,128)}, f32[768,1536]{1,0:T(8,128)}), (f32[384,6448]{0,1:T(8,128)}, f32[768,1536]{1,0:T(8,128)})) %all-reduce.50.cloned.1.call-update) | async-done | bytes 14622736 | tf_op jit(solution)/shard_map/psum | solution.py:205
  2139.6 8.5 copy.732
  (637 shorter events, 468.9 us)
Async XLA Ops:
  7.2 576.0 %all-gather.6.cloned.1.call-start = ((), (), s32[]{:S(2)}) async-start(), calls=%async_computation.3 | async-start | bytes 11796480 | tf_op jit(solution)/shard_map/all_gather | solution.py:136
  7.2 107.6 %collective-permute-start = (bf16[384,6448]{0,1:T(8,128)(2,1)}, bf16[384,6448]{0,1:T(8,128)(2,1)}, u32[]{:S(2)}, u32[]{:S(2)}) collective-permute-start(bf16[384,6448]{0,1:T(8,128)(2,1)} %param.13), channel_id=1, source_target_pairs={{0,8},{8,16},{16,24},{24,0},{1,9},{9,17},{17,25},{25,1},{2,10},{10... | collective-permute-start | bytes 14856200 | tf_op jit(solution)/shard_map/ppermute | solution.py:114
  7.8 261.3 %collective-permute-start.1 = (bf16[384,6448]{0,1:T(8,128)(2,1)}, bf16[384,6448]{0,1:T(8,128)(2,1)}, u32[]{:S(2)}, u32[]{:S(2)}) collective-permute-start(bf16[384,6448]{0,1:T(8,128)(2,1)} %param.13), channel_id=1, source_target_pairs={{0,24},{8,0},{16,8},{24,16},{1,25},{9,1},{17,9},{25,17},{2,26},{10... | collective-permute-start | bytes 14856200 | tf_op jit(solution)/shard_map/ppermute | solution.py:119
  114.8 159.8 %collective-permute-start.2 = (bf16[384,6448]{0,1:T(8,128)(2,1)}, bf16[384,6448]{0,1:T(8,128)(2,1)}, u32[]{:S(2)}, u32[]{:S(2)}) collective-permute-start(bf16[384,6448]{0,1:T(8,128)(2,1)} %collective-permute-done), channel_id=1, source_target_pairs={{0,8},{8,16},{16,24},{24,0},{1,9},{9,17},{17,25},{25,1},{2,10},{10... | collective-permute-start | bytes 14856200 | tf_op jit(solution)/shard_map/ppermute | solution.py:114
  117.2 1139.1 %reduce-scatter.8.cloned.1.call-start = ((), (), s32[]{:S(2)}) async-start(), calls=%async_computation.6 | async-start | bytes 23592960 | tf_op jit(solution)/shard_map/reduce_scatter | solution.py:203
  222.6 57.4 %copy-start.124 = (f32[1536]{0:T(1024)}, f32[1536]{0:T(1024)S(1)}, u32[]{:S(2)}) copy-start(f32[1536]{0:T(1024)S(1)} %reshape.1986) | copy-start | bytes 18436
  236.5 72.8 %copy-start.133 = (f32[48]{0:T(128)}, f32[48]{0:T(128)S(1)}, u32[]{:S(2)}) copy-start(f32[48]{0:T(128)S(1)} %convert_element_type.66) | copy-start | bytes 580
  250.6 60.0 %copy-start.119 = (f32[48]{0:T(128)}, f32[48]{0:T(128)S(1)}, u32[]{:S(2)}) copy-start(f32[48]{0:T(128)S(1)} %fusion.296) | copy-start | bytes 580
  342.5 30.9 %copy-start.95 = (f32[48,2]{1,0:T(8,128)S(1)}, f32[48,2]{1,0:T(8,128)}, u32[]{:S(2)}) copy-start(f32[48,2]{1,0:T(8,128)} %copy.584) | copy-start | bytes 1156
  342.5 31.7 %copy-start.82 = (f32[1,48,2,128]{3,2,0,1:T(2,128)S(1)}, f32[1,48,2,128]{3,2,0,1:T(2,128)}, u32[]{:S(2)}) copy-start(f32[1,48,2,128]{3,2,0,1:T(2,128)} %copy.589) | copy-start | bytes 147460
  452.9 323.4 %copy-start.1 = (f32[48,64,128]{2,1,0:T(8,128)}, f32[48,64,128]{2,1,0:T(8,128)S(1)}, u32[]{:S(2)}) copy-start(f32[48,64,128]{2,1,0:T(8,128)S(1)} %convolution_add_fusion) | copy-start | bytes 4718596
  458.1 300.5 %copy-start.3 = (f32[48,64,128]{2,1,0:T(8,128)}, f32[48,64,128]{2,1,0:T(8,128)S(1)}, u32[]{:S(2)}) copy-start(f32[48,64,128]{2,1,0:T(8,128)S(1)} %multiply_add_fusion.2) | copy-start | bytes 4718596
  563.6 42.0 %copy-start.126 = (f32[1024]{0:T(1024)}, f32[1024]{0:T(1024)S(1)}, u32[]{:S(2)}) copy-start(f32[1024]{0:T(1024)S(1)} %fusion.295) | copy-start | bytes 12292
  565.8 104.8 %copy-start.44 = (f32[1,256,128]{2,1,0:T(8,128)}, f32[1,256,128]{2,1,0:T(8,128)S(1)}, u32[]{:S(2)}) copy-start(f32[1,256,128]{2,1,0:T(8,128)S(1)} %get-tuple-element.42) | copy-start | bytes 393220
  565.8 135.9 %copy-start.41 = (f32[1,256,128]{2,1,0:T(8,128)}, f32[1,256,128]{2,1,0:T(8,128)S(1)}, u32[]{:S(2)}) copy-start(f32[1,256,128]{2,1,0:T(8,128)S(1)} %get-tuple-element.54) | copy-start | bytes 393220
  583.1 939.7 %reduce-scatter.6.cloned.1.call-start = ((), (), s32[]{:S(2)}) async-start(), calls=%async_computation.5 | async-start | bytes 49520640 | tf_op jit(solution)/shard_map/reduce_scatter | solution.py:196
  835.6 43.1 %copy-start.106 = (f32[48,256]{1,0:T(8,128)}, f32[48,256]{1,0:T(8,128)S(1)}, u32[]{:S(2)}) copy-start(f32[48,256]{1,0:T(8,128)S(1)} %bitcast_add_fusion.28) | copy-start | bytes 147460
  836.5 42.3 %copy-start.104 = (f32[48,256]{1,0:T(8,128)}, f32[48,256]{1,0:T(8,128)S(1)}, u32[]{:S(2)}) copy-start(f32[48,256]{1,0:T(8,128)S(1)} %bitcast_add_fusion.27) | copy-start | bytes 147460
  837.3 41.4 %copy-start.102 = (f32[48,256]{1,0:T(8,128)}, f32[48,256]{1,0:T(8,128)S(1)}, u32[]{:S(2)}) copy-start(f32[48,256]{1,0:T(8,128)S(1)} %bitcast_add_fusion.26) | copy-start | bytes 147460
  837.7 41.0 %copy-start.79 = (f32[256,256]{1,0:T(8,128)}, f32[256,256]{1,0:T(8,128)S(1)}, u32[]{:S(2)}) copy-start(f32[256,256]{1,0:T(8,128)S(1)} %fusion.255) | copy-start | bytes 786436
  838.1 40.6 %copy-start.77 = (f32[256,256]{1,0:T(8,128)}, f32[256,256]{1,0:T(8,128)S(1)}, u32[]{:S(2)}) copy-start(f32[256,256]{1,0:T(8,128)S(1)} %fusion.244) | copy-start | bytes 786436
  838.5 40.3 %copy-start.76 = (f32[256,256]{1,0:T(8,128)}, f32[256,256]{1,0:T(8,128)S(1)}, u32[]{:S(2)}) copy-start(f32[256,256]{1,0:T(8,128)S(1)} %fusion.233) | copy-start | bytes 786436
  878.9 46.3 %copy-start.20 = (f32[48,64,128]{2,1,0:T(8,128)S(1)}, f32[48,64,128]{2,1,0:T(8,128)}, u32[]{:S(2)}) copy-start(f32[48,64,128]{2,1,0:T(8,128)} %copy-done.19) | copy-start | bytes 4718596
  878.9 46.3 %copy-start.45 = (f32[1,256,128]{2,1,0:T(8,128)S(1)}, f32[1,256,128]{2,1,0:T(8,128)}, u32[]{:S(2)}) copy-start(f32[1,256,128]{2,1,0:T(8,128)} %copy-done.44) | copy-start | bytes 393220
  878.9 49.0 %copy-start.71 = (f32[1,256,48]{1,0,2:T(1,128)S(1)}, f32[1,256,48]{1,0,2:T(1,128)}, u32[]{:S(2)}) copy-start(f32[1,256,48]{1,0,2:T(1,128)} %copy-done.70) | copy-start | bytes 147460
  878.9 59.5 %copy-start.51 = (f32[1,48,256]{1,2,0:T(8,128)S(1)}, f32[1,48,256]{1,2,0:T(8,128)}, u32[]{:S(2)}) copy-start(f32[1,48,256]{1,2,0:T(8,128)} %copy-done.50) | copy-start | bytes 147460
  878.9 59.5 %copy-start.37 = (f32[1,256,48]{2,1,0:T(8,128)S(1)}, f32[1,256,48]{2,1,0:T(8,128)}, u32[]{:S(2)}) copy-start(f32[1,256,48]{2,1,0:T(8,128)} %get-tuple-element.49) | copy-start | bytes 147460
  878.9 60.5 %copy-start.4 = (f32[48,64,128]{2,1,0:T(8,128)S(1)}, f32[48,64,128]{2,1,0:T(8,128)}, u32[]{:S(2)}) copy-start(f32[48,64,128]{2,1,0:T(8,128)} %copy-done.3) | copy-start | bytes 4718596
  1080.9 28.9 %copy-start.55 = (f32[1,256,128]{2,1,0:T(8,128)S(1)}, f32[1,256,128]{2,1,0:T(8,128)}, u32[]{:S(2)}) copy-start(f32[1,256,128]{2,1,0:T(8,128)} %get-tuple-element.53) | copy-start | bytes 393220
  1080.9 28.9 %copy-start.66 = (f32[256,256]{1,0:T(8,128)S(1)}, f32[256,256]{1,0:T(8,128)}, u32[]{:S(2)}) copy-start(f32[256,256]{1,0:T(8,128)} %get-tuple-element.98) | copy-start | bytes 786436
  1110.3 27.1 %slice-start = ((s8[12582912]{0:T(1024)(128)(4,1)}), s8[4194304]{0:T(1024)(128)(4,1)S(1)}, s32[]{:S(2)}) async-start(s8[12582912]{0:T(1024)(128)(4,1)} %bitcast.941), calls=%async_computation.9 | async-start | bytes 8388608
  1147.5 36.2 %copy-start.91 = (f32[3328]{0:T(1024)S(1)}, f32[3328]{0:T(1024)}, u32[]{:S(2)}) copy-start(f32[3328]{0:T(1024)} %get-tuple-element.110) | copy-start | bytes 39940
  1147.5 36.2 %copy-start.92 = (f32[3328]{0:T(1024)S(1)}, f32[3328]{0:T(1024)}, u32[]{:S(2)}) copy-start(f32[3328]{0:T(1024)} %get-tuple-element.111) | copy-start | bytes 39940
  1147.5 36.2 %copy-start.93 = (f32[3328]{0:T(1024)S(1)}, f32[3328]{0:T(1024)}, u32[]{:S(2)}) copy-start(f32[3328]{0:T(1024)} %get-tuple-element.112) | copy-start | bytes 39940
  1147.5 36.2 %copy-start.94 = (f32[3328]{0:T(1024)S(1)}, f32[3328]{0:T(1024)}, u32[]{:S(2)}) copy-start(f32[3328]{0:T(1024)} %get-tuple-element.113) | copy-start | bytes 39940
  1253.7 301.0 %reduce-scatter.10.cloned.1.call-start = ((), (), s32[]{:S(2)}) async-start(), calls=%async_computation.7 | async-start | bytes 2129920
  1255.6 269.8 %copy-start.118 = (f32[3072]{0:T(1024)S(1)}, f32[3072]{0:T(1024)}, u32[]{:S(2)}) copy-start(f32[3072]{0:T(1024)} %get-tuple-element.133) | copy-start | bytes 36868
  1255.6 270.0 %copy-start.136 = (f32[48]{0:T(128)S(1)}, f32[48]{0:T(128)}, u32[]{:S(2)}) copy-start(f32[48]{0:T(128)} %get-tuple-element.201) | copy-start | bytes 580
  1255.6 270.0 %copy-start.137 = (f32[48]{0:T(128)S(1)}, f32[48]{0:T(128)}, u32[]{:S(2)}) copy-start(f32[48]{0:T(128)} %get-tuple-element.199) | copy-start | bytes 580
  1255.7 270.0 %copy-start.139 = (bf16[48]{0:T(256)(128)(2,1)S(1)}, bf16[48]{0:T(256)(128)(2,1)}, u32[]{:S(2)}) copy-start(bf16[48]{0:T(256)(128)(2,1)} %copy-done.138) | copy-start | bytes 292
  1255.7 270.0 %copy-start.117 = (f32[4,1,768]{2,1,0:T(1,128)S(1)}, f32[4,1,768]{2,1,0:T(1,128)}, u32[]{:S(2)}) copy-start(f32[4,1,768]{2,1,0:T(1,128)} %convert_element_type.82) | copy-start | bytes 36868
  1255.7 270.0 %copy-start.127 = (f32[1024]{0:T(1024)S(1)}, f32[1024]{0:T(1024)}, u32[]{:S(2)}) copy-start(f32[1024]{0:T(1024)} %copy-done.126) | copy-start | bytes 12292
  1255.7 425.3 %all-gather.8.cloned.1.call-start = ((), (), s32[]{:S(2)}) async-start(), calls=%async_computation.4 | async-start | bytes 24760320 | tf_op jit(solution)/shard_map/all_gather | solution.py:174
  1256.3 883.3 %all-reduce.50.cloned.1.call-start = ((), (), s32[]{:S(2)}) async-start(), calls=%async_computation.8 | async-start | bytes 29245440 | tf_op jit(solution)/shard_map/psum | solution.py:205
  1555.8 157.3 %copy-start.98 = (f32[3328]{0:T(1024)S(1)}, f32[3328]{0:T(1024)}, u32[]{:S(2)}) copy-start(f32[3328]{0:T(1024)} %get-tuple-element.78) | copy-start | bytes 39940
  1555.8 157.3 %copy-start.130 = (f32[3072]{0:T(1024)S(1)}, f32[3072]{0:T(1024)}, u32[]{:S(2)}) copy-start(f32[3072]{0:T(1024)} %get-tuple-element.76) | copy-start | bytes 36868
  1555.8 157.3 %copy-start.135 = (f32[48]{0:T(128)S(1)}, f32[48]{0:T(128)}, u32[]{:S(2)}) copy-start(f32[48]{0:T(128)} %get-tuple-element.135) | copy-start | bytes 580
  1555.8 209.5 %copy-start.123 = (f32[1024]{0:T(1024)S(1)}, f32[1024]{0:T(1024)}, u32[]{:S(2)}) copy-start(f32[1024]{0:T(1024)} %copy-done.122) | copy-start | bytes 12292
  (106 other events, 1475.6 us)
Sparse Core Ops, SparseCore 0:
  117.4 91.3 all-gather.5
  583.2 137.3 reduce-scatter.7
  1253.8 268.9 reduce-scatter.5
  1525.8 28.7 reduce-scatter.9
  1556.1 124.8 all-gather.7
  1685.1 454.4 all-reduce.49
